TPU v7x, 256 devices: a whole 4x4x8 slice. The times are simulated.
256 devices in a mesh: samp: 16 (over z, core), feat: 16 (over x, y).
Axes of the slice: x: 4, y: 4, z: 8, core: 2. Of those that a mesh axis runs over, the one named last changes fastest.
Arguments:
- differences: bfloat16 [9216, 131072], P('samp', 'feat'), may hold values from -600 to 600
- start_block: bfloat16 [64, 131072], P(None, 'feat'), may hold values from -6 to 6
Outputs:
- directions: float32 [64, 131072], P(None, 'feat')
- layer_scores: float32 [16, 64], P('feat')
All inputs are finite; a program needn't handle non-finite values.
Results may differ from a plain program's by a relative error of at most 0.0043.
Values may be sent and summed in bfloat16 or wider, within the bound.
A program may use at most 64 MiB of HBM per device.

v0:
```python
import math
import jax
import jax.numpy as jnp
from jax import lax
from jax.sharding import PartitionSpec as P

WIDTH = 8192
ITERS = 2
FEATURES = 131072


def orthonormal(pulled, gram):
    lower = jnp.linalg.cholesky(gram)
    return lax.linalg.triangular_solve(lower, pulled, left_side=True, lower=True)


def on_device(differences, start_block):
    block = start_block
    basis = None
    for step in range(ITERS):
        partial_rows = lax.dot_general(
            block, differences, (((1,), (1,)), ((), ())), preferred_element_type=jnp.float32
        )
        projected = lax.psum(partial_rows, "feat").astype(jnp.bfloat16)
        partial_cols = jnp.dot(projected, differences, preferred_element_type=jnp.float32)
        pulled = lax.psum(partial_cols, "samp")
        local_gram = jnp.dot(pulled, pulled.T, precision=lax.Precision.HIGHEST)
        gram = lax.psum(local_gram, "feat")
        basis = orthonormal(pulled, gram)
        block = basis.astype(jnp.bfloat16)
    directions = basis * math.sqrt(FEATURES)
    samples = differences.shape[0]
    layers_here = differences.shape[1] // WIDTH
    stacked = differences.reshape(samples, layers_here, WIDTH)
    block_layers = block.reshape(block.shape[0], layers_here, WIDTH)
    along = jnp.einsum("kjw,sjw->jks", block_layers, stacked, preferred_element_type=jnp.float32)
    captured = jnp.sum(along * along, axis=2)
    energy = jnp.einsum("sjw,sjw->j", stacked, stacked, preferred_element_type=jnp.float32)
    captured, energy = lax.psum((captured, energy), "samp")
    layer_scores = FEATURES * captured / (energy[:, None] + 1e-06)
    return (directions, layer_scores)


def solution(mesh):
    in_specs = (P("samp", "feat"), P(None, "feat"))
    out_specs = (P(None, "feat"), P("feat", None))
    return jax.shard_map(
        on_device, mesh=mesh, in_specs=in_specs, out_specs=out_specs, check_vma=False
    )
```

profile of v0, /device:TPU:1, one launch (start us, length us, event | category | flops | bytes accessed | tf_op | source)
XLA Modules:
  0.0 635.0 jit_solution(9600654586622632830)
XLA Ops:
  7.2 0.0 all-reduce.6.cloned.1.call-start
  7.2 1.2 copy-done
  8.4 6.6 %fusion.16 = f32[64,576]{1,0:T(8,128)S(1)} fusion(bf16[64,8192]{1,0:T(8,128)(2,1)S(1)} %copy-done, bf16[576,8192]{1,0:T(8,128)(2,1)} %param.5), kind=kOutput, calls=%fused_computation.30 | convolution fusion | flops 603979776 | bytes 10633216 | tf_op jit(solution)/shard_map/dot_general | solution.py:21
  15.0 63.0 %all-reduce.9 = bf16[64,576]{1,0:T(8,128)(2,1)S(1)} all-reduce(f32[64,576]{1,0:T(8,128)S(1)} %fusion.16), channel_id=1, replica_groups=mesh['samp'=16,'feat'=16] {'feat'}, use_global_device_ids=true, to_apply=%region_0.0 | all-reduce | flops 36864 | bytes 221184 | tf_op jit(solution)/shard_map/psum | solution.py:24
  77.9 6.9 %fusion.21 = f32[64,8192]{1,0:T(8,128)} fusion(bf16[64,576]{1,0:T(8,128)(2,1)S(1)} %all-reduce.9, bf16[576,8192]{1,0:T(8,128)(2,1)} %param.5), kind=kOutput, calls=%fused_computation.35 | convolution fusion | flops 603979776 | bytes 11608064 | tf_op jit(solution)/shard_map/dot_general | solution.py:25
  84.9 0.0 all-reduce.8.cloned.1.call-start
  84.9 127.8 %all-reduce.6.cloned.1.call-done = f32[64,8192]{1,0:T(8,128)} async-done(((f32[64,8192]{1,0:T(8,128)}), f32[64,8192]{1,0:T(8,128)}) %all-reduce.6.cloned.1.call-update) | async-done | bytes 2097168 | tf_op jit(solution)/shard_map/psum | solution.py:26
  212.7 4.2 fusion.17
  216.9 60.3 %psum.58 = f32[64,64]{0,1:T(8,128)S(1)} all-reduce(f32[64,64]{0,1:T(8,128)S(1)} %fusion.17), channel_id=1, replica_groups=mesh['samp'=16,'feat'=16] {'feat'}, use_global_device_ids=true, to_apply=%region_2.0 | all-reduce | flops 4096 | bytes 32768 | tf_op jit(solution)/shard_map/psum | solution.py:28
  277.1 0.1 copy.5
  277.2 5.8 cholesky.44
  283.1 0.6 compare_reduce_fusion.1
  283.8 0.7 fusion.7
  284.4 4.9 custom-call.6
  289.3 1.9 convolution_convert_fusion
  291.2 6.6 %fusion.18 = f32[64,576]{1,0:T(8,128)S(1)} fusion(bf16[64,8192]{1,0:T(8,128)(2,1)S(1)} %convolution_convert_fusion, bf16[576,8192]{1,0:T(8,128)(2,1)} %param.5), kind=kOutput, calls=%fused_computation.32 | convolution fusion | flops 603979776 | bytes 10633216 | tf_op jit(solution)/shard_map/dot_general | solution.py:21
  297.8 57.4 %all-reduce.10 = bf16[64,576]{1,0:T(8,128)(2,1)S(1)} all-reduce(f32[64,576]{1,0:T(8,128)S(1)} %fusion.18), channel_id=1, replica_groups=mesh['samp'=16,'feat'=16] {'feat'}, use_global_device_ids=true, to_apply=%region_5.8 | all-reduce | flops 36864 | bytes 221184 | tf_op jit(solution)/shard_map/psum | solution.py:24
  355.3 6.9 %fusion.20 = f32[64,8192]{1,0:T(8,128)} fusion(bf16[64,576]{1,0:T(8,128)(2,1)S(1)} %all-reduce.10, bf16[576,8192]{1,0:T(8,128)(2,1)} %param.5), kind=kOutput, calls=%fused_computation.34 | convolution fusion | flops 603979776 | bytes 11608064 | tf_op jit(solution)/shard_map/dot_general | solution.py:25
  362.2 0.0 all-reduce.8.cloned.1.call-update
  362.2 9.1 %fusion = f32[]{:T(128)} fusion(bf16[576,8192]{1,0:T(8,128)(2,1)} %param.5), kind=kLoop, calls=%fused_computation.1 | loop fusion | flops 14155775 | bytes 9437188 | tf_op jit(solution)/shard_map/sjw,sjw->j/dot_general | solution.py:38
  371.4 130.6 %all-reduce.8.cloned.1.call-done = f32[64,8192]{1,0:T(8,128)} async-done(((f32[64,8192]{1,0:T(8,128)}), f32[64,8192]{1,0:T(8,128)}) %all-reduce.8.cloned.1.call-update) | async-done | bytes 2097168 | tf_op jit(solution)/shard_map/psum | solution.py:26
  502.0 4.2 fusion.19
  506.1 60.3 %psum.61 = f32[64,64]{0,1:T(8,128)S(1)} all-reduce(f32[64,64]{0,1:T(8,128)S(1)} %fusion.19), channel_id=1, replica_groups=mesh['samp'=16,'feat'=16] {'feat'}, use_global_device_ids=true, to_apply=%region_7.10 | all-reduce | flops 4096 | bytes 32768 | tf_op jit(solution)/shard_map/psum | solution.py:28
  566.4 0.1 copy.7
  566.5 5.8 cholesky.55
  572.4 0.6 compare_reduce_fusion
  573.0 0.7 fusion.8
  573.7 4.9 custom-call.7
  578.6 3.3 broadcast_multiply_fusion
  581.9 6.7 %fusion.1 = f32[64]{0:T(128)S(1)} fusion(bf16[576,8192]{1,0:T(8,128)(2,1)} %param.5, bf16[64,8192]{1,0:T(8,128)(2,1)S(1)} %get-tuple-element.7), kind=kOutput, calls=%fused_computation.4 | convolution fusion | flops 604053440 | bytes 10486016 | tf_op jit(solution)/shard_map/kjw,sjw->jks/dot_general | solution.py:36
  588.6 38.4 %all-reduce = (f32[1,64]{1,0:T(1,128)S(1)}, f32[1]{0:T(128)}) all-reduce(f32[1,64]{1,0:T(1,128)S(1)} %bitcast.39, f32[1]{0:T(128)} %bitcast.7), channel_id=1, replica_groups=mesh['samp'=16,'feat'=16] {'samp'}, use_global_device_ids=true, to_apply=%region_9.12 | all-reduce | flops 65 | bytes 520 | tf_op jit(solution)/shard_map/psum | solution.py:39
  627.6 0.5 multiply_divide_fusion
  (10 shorter events, 0.1 us)
Async XLA Ops:
  7.2 1.2 copy-start
  7.2 205.5 %all-reduce.6.cloned.1.call-start = ((), (), s32[]{:S(2)}) async-start(), calls=%async_computation | async-start | bytes 4194304 | tf_op jit(solution)/shard_map/psum | solution.py:26
  84.9 417.1 %all-reduce.8.cloned.1.call-start = ((), (), s32[]{:S(2)}) async-start(), calls=%async_computation.1 | async-start | bytes 4194304 | tf_op jit(solution)/shard_map/psum | solution.py:26
  212.7 76.6 %copy-start.2 = (f32[64,8192]{1,0:T(8,128)S(1)}, f32[64,8192]{1,0:T(8,128)}, u32[]{:S(2)}) copy-start(f32[64,8192]{1,0:T(8,128)} %all-reduce.6.cloned.1.call-done) | copy-start | bytes 6291460
  502.0 76.6 %copy-start.1 = (f32[64,8192]{1,0:T(8,128)S(1)}, f32[64,8192]{1,0:T(8,128)}, u32[]{:S(2)}) copy-start(f32[64,8192]{1,0:T(8,128)} %all-reduce.8.cloned.1.call-done) | copy-start | bytes 6291460
Sparse Core Ops, SparseCore 0:
  85.0 127.6 all-reduce.5
  362.3 139.5 all-reduce.7
where the time goes:
time: 635 us
  blocking collectives  279 us (44%)
  waiting for transfers between devices  258 us (41%)
  matrix products  47.2 us (7%)
  other arithmetic  33.8 us (5%)
  between operations  14.8 us (2%)
    psum x2, waiting for transfers between devices, on_device(): pulled = lax.psum(partial_cols, 'samp')  258 us
    psum x2, blocking collectives, on_device(): gram = lax.psum(local_gram, 'feat')  121 us
    psum x2, blocking collectives, on_device(): projected = lax.psum(partial_rows, 'feat').astype(jnp.bfloat16)  120 us
    psum x1, blocking collectives, on_device(): captured, energy = lax.psum((captured, energy), 'samp')  38.4 us
    dot_general x2, matrix products, on_device(): jnp.dot(projected, differences, preferred_element_type=jnp.float32)  13.8 us
    dot_general x2, matrix products, on_device(): lax.dot_general(block, differences, (((1,), (1,)), ((), ())), preferred_e...  13.2 us
    another operation x6, other arithmetic, orthonormal(): lower = jnp.linalg.cholesky(gram)  13 us
  transfers between devices with their start and end apart: 2, of which 2 were waited for; matrix products, arithmetic and copies ran while one was open for 1% of the time, Pallas kernels for 0%

commit v1 on v0

--- a/solution.py
+++ b/solution.py
@@ -7,6 +7,14 @@
 WIDTH = 8192
 ITERS = 2
 FEATURES = 131072
+
+
+def sum_by_hops(x, axis):
+    count, summed = (lax.axis_size(axis), x)
+    for far in [1 << k for k in range(count.bit_length() - 1)]:
+        swap = [(i, i ^ far) for i in range(count)]
+        summed = summed + lax.ppermute(summed, axis, swap)
+    return summed
 
 
 def orthonormal(pulled, gram):
@@ -23,7 +31,7 @@
         )
         projected = lax.psum(partial_rows, "feat").astype(jnp.bfloat16)
         partial_cols = jnp.dot(projected, differences, preferred_element_type=jnp.float32)
-        pulled = lax.psum(partial_cols, "samp")
+        pulled = sum_by_hops(partial_cols, "samp")
         local_gram = jnp.dot(pulled, pulled.T, precision=lax.Precision.HIGHEST)
         gram = lax.psum(local_gram, "feat")
         basis = orthonormal(pulled, gram)

time: 635 us -> 867 us (1.37)
  waiting for transfers between devices: 258 us -> 459 us
  starting transfers between devices: 0.08 us -> 61.6 us
  between operations: 14.8 us -> 1.49 us
    ppermute x0 -> x8, waiting for transfers between devices: none -> 459 us  [sum_by_hops(): summed = summed + lax.ppermute(summed, axis, swap)]
    psum x2 -> x0, waiting for transfers between devices: 258 us -> none  [on_device(): pulled = lax.psum(partial_cols, 'samp')]
    ppermute x0 -> x8, starting transfers between devices: none -> 61.6 us  [sum_by_hops(): summed = summed + lax.ppermute(summed, axis, swap)]
  transfers between devices with their start and end apart: 2 -> 8, of which waited for: 2 -> 8; matrix products, arithmetic and copies ran while one was open for 1% -> 1% of each run, Pallas kernels for 0% -> 0%
where the time goes in v1:
time: 867 us
  waiting for transfers between devices  459 us (53%)
  blocking collectives  272 us (31%)
  starting transfers between devices  61.6 us (7%)
  matrix products  39.9 us (5%)
  other arithmetic  31.9 us (4%)
    ppermute x8, waiting for transfers between devices, sum_by_hops(): summed = summed + lax.ppermute(summed, axis, swap)  459 us
    psum x2, blocking collectives, on_device(): projected = lax.psum(partial_rows, 'feat').astype(jnp.bfloat16)  120 us
    psum x2, blocking collectives, on_device(): gram = lax.psum(local_gram, 'feat')  113 us
    ppermute x8, starting transfers between devices, sum_by_hops(): summed = summed + lax.ppermute(summed, axis, swap)  61.6 us
    psum x1, blocking collectives, on_device(): captured, energy = lax.psum((captured, energy), 'samp')  38.3 us
  transfers between devices with their start and end apart: 8, of which 8 were waited for; matrix products, arithmetic and copies ran while one was open for 1% of the time, Pallas kernels for 0%

profile of v1, /device:TPU:1, one launch (start us, length us, event | category | flops | bytes accessed | tf_op | source)
XLA Modules:
  0.0 866.5 jit_solution(13082511426058333922)
XLA Ops:
  1.9 6.6 fusion.16
  8.4 63.0 %all-reduce.3 = bf16[64,576]{1,0:T(8,128)(2,1)S(1)} all-reduce(f32[64,576]{1,0:T(8,128)S(1)} %fusion.16), channel_id=1, replica_groups=mesh['samp'=16,'feat'=16] {'feat'}, use_global_device_ids=true, to_apply=%region_0.0 | all-reduce | flops 36864 | bytes 221184 | tf_op jit(solution)/shard_map/psum | solution.py:32
  71.4 5.6 fusion.21
  77.0 15.0 %collective-permute-start = (f32[64,8192]{1,0:T(8,128)S(1)}, f32[64,8192]{1,0:T(8,128)S(1)}, u32[]{:S(2)}, u32[]{:S(2)}) collective-permute-start(f32[64,8192]{1,0:T(8,128)S(1)} %fusion.21), channel_id=1, source_target_pairs={{0,16},{16,0},{32,48},{48,32},{64,80},{80,64},{96,112},{112,96},{1... | collective-permute-start | bytes 6291464 | tf_op jit(solution)/shard_map/ppermute | solution.py:16
  92.0 3.8 collective-permute-done
  97.7 45.6 %collective-permute-done.1 = f32[64,8192]{1,0:T(8,128)S(1)} collective-permute-done((f32[64,8192]{1,0:T(8,128)S(1)}, f32[64,8192]{1,0:T(8,128)S(1)}, u32[]{:S(2)}, u32[]{:S(2)}) %collective-permute-start.1) | collective-permute-done | bytes 2097184 | tf_op jit(solution)/shard_map/ppermute | solution.py:16
  143.6 3.1 collective-permute-start.2
  146.6 90.0 %collective-permute-done.2 = f32[64,8192]{1,0:T(8,128)S(1)} collective-permute-done((f32[64,8192]{1,0:T(8,128)S(1)}, f32[64,8192]{1,0:T(8,128)S(1)}, u32[]{:S(2)}, u32[]{:S(2)}) %collective-permute-start.2) | collective-permute-done | bytes 2097184 | tf_op jit(solution)/shard_map/ppermute | solution.py:16
  236.8 6.5 collective-permute-start.3
  243.3 90.5 %collective-permute-done.3 = f32[64,8192]{1,0:T(8,128)S(1)} collective-permute-done((f32[64,8192]{1,0:T(8,128)S(1)}, f32[64,8192]{1,0:T(8,128)S(1)}, u32[]{:S(2)}, u32[]{:S(2)}) %collective-permute-start.3) | collective-permute-done | bytes 2097184 | tf_op jit(solution)/shard_map/ppermute | solution.py:16
  335.8 55.8 %psum.43 = f32[64,64]{0,1:T(8,128)S(1)} all-reduce(f32[64,64]{0,1:T(8,128)S(1)} %fusion.17), channel_id=1, replica_groups=mesh['samp'=16,'feat'=16] {'feat'}, use_global_device_ids=true, to_apply=%region_1.0 | all-reduce | flops 4096 | bytes 32768 | tf_op jit(solution)/shard_map/psum | solution.py:36
  391.7 5.8 cholesky.44
  398.9 4.9 custom-call.6
  403.8 1.9 convolution_convert_fusion
  405.7 6.6 fusion.18
  412.3 57.2 %all-reduce.4 = bf16[64,576]{1,0:T(8,128)(2,1)S(1)} all-reduce(f32[64,576]{1,0:T(8,128)S(1)} %fusion.18), channel_id=1, replica_groups=mesh['samp'=16,'feat'=16] {'feat'}, use_global_device_ids=true, to_apply=%region_4.7 | all-reduce | flops 36864 | bytes 221184 | tf_op jit(solution)/shard_map/psum | solution.py:32
  469.5 5.7 fusion.20
  475.3 29.6 %collective-permute-start.4 = (f32[64,8192]{1,0:T(8,128)S(1)}, f32[64,8192]{1,0:T(8,128)S(1)}, u32[]{:S(2)}, u32[]{:S(2)}) collective-permute-start(f32[64,8192]{1,0:T(8,128)S(1)} %fusion.20), channel_id=1, source_target_pairs={{0,16},{16,0},{32,48},{48,32},{64,80},{80,64},{96,112},{112,96},{1... | collective-permute-start | bytes 6291464 | tf_op jit(solution)/shard_map/ppermute | solution.py:16
  504.9 3.8 collective-permute-done.4
  509.0 46.8 %collective-permute-done.5 = f32[64,8192]{1,0:T(8,128)S(1)} collective-permute-done((f32[64,8192]{1,0:T(8,128)S(1)}, f32[64,8192]{1,0:T(8,128)S(1)}, u32[]{:S(2)}, u32[]{:S(2)}) %collective-permute-start.5) | collective-permute-done | bytes 2097184 | tf_op jit(solution)/shard_map/ppermute | solution.py:16
  556.0 2.0 collective-permute-start.6
  558.0 91.0 %collective-permute-done.6 = f32[64,8192]{1,0:T(8,128)S(1)} collective-permute-done((f32[64,8192]{1,0:T(8,128)S(1)}, f32[64,8192]{1,0:T(8,128)S(1)}, u32[]{:S(2)}, u32[]{:S(2)}) %collective-permute-start.6) | collective-permute-done | bytes 2097184 | tf_op jit(solution)/shard_map/ppermute | solution.py:16
  649.2 3.7 collective-permute-start.7
  652.9 5.5 fusion
  658.4 87.2 %collective-permute-done.7 = f32[64,8192]{1,0:T(8,128)S(1)} collective-permute-done((f32[64,8192]{1,0:T(8,128)S(1)}, f32[64,8192]{1,0:T(8,128)S(1)}, u32[]{:S(2)}, u32[]{:S(2)}) %collective-permute-start.7) | collective-permute-done | bytes 2097184 | tf_op jit(solution)/shard_map/ppermute | solution.py:16
  745.8 1.8 fusion.19
  747.6 57.3 %psum.45 = f32[64,64]{0,1:T(8,128)S(1)} all-reduce(f32[64,64]{0,1:T(8,128)S(1)} %fusion.19), channel_id=1, replica_groups=mesh['samp'=16,'feat'=16] {'feat'}, use_global_device_ids=true, to_apply=%region_5.8 | all-reduce | flops 4096 | bytes 32768 | tf_op jit(solution)/shard_map/psum | solution.py:36
  805.0 5.8 cholesky.55
  812.2 4.9 custom-call.7
  817.1 3.3 broadcast_multiply_fusion
  820.3 6.7 fusion.1
  827.0 38.3 %all-reduce = (f32[1,64]{1,0:T(1,128)S(1)}, f32[1]{0:T(128)}) all-reduce(f32[1,64]{1,0:T(1,128)S(1)} %bitcast.41, f32[1]{0:T(128)} %bitcast.7), channel_id=1, replica_groups=mesh['samp'=16,'feat'=16] {'samp'}, use_global_device_ids=true, to_apply=%region_7.10 | all-reduce | flops 65 | bytes 520 | tf_op jit(solution)/shard_map/psum | solution.py:47
  (31 shorter events, 9.9 us)
Async XLA Ops:
  0.6 1.2 copy-start
  77.0 18.7 %collective-permute-start = (f32[64,8192]{1,0:T(8,128)S(1)}, f32[64,8192]{1,0:T(8,128)S(1)}, u32[]{:S(2)}, u32[]{:S(2)}) collective-permute-start(f32[64,8192]{1,0:T(8,128)S(1)} %fusion.21), channel_id=1, source_target_pairs={{0,16},{16,0},{32,48},{48,32},{64,80},{80,64},{96,112},{112,96},{1... | collective-permute-start | bytes 6291464 | tf_op jit(solution)/shard_map/ppermute | solution.py:16
  96.0 47.4 %collective-permute-start.1 = (f32[64,8192]{1,0:T(8,128)S(1)}, f32[64,8192]{1,0:T(8,128)S(1)}, u32[]{:S(2)}, u32[]{:S(2)}) collective-permute-start(f32[64,8192]{1,0:T(8,128)S(1)} %add.48), channel_id=1, source_target_pairs={{0,32},{16,48},{32,0},{48,16},{64,96},{80,112},{96,64},{112,80},{1... | collective-permute-start | bytes 6291464 | tf_op jit(solution)/shard_map/ppermute | solution.py:16
  143.6 93.1 %collective-permute-start.2 = (f32[64,8192]{1,0:T(8,128)S(1)}, f32[64,8192]{1,0:T(8,128)S(1)}, u32[]{:S(2)}, u32[]{:S(2)}) collective-permute-start(f32[64,8192]{1,0:T(8,128)S(1)} %add.49), channel_id=1, source_target_pairs={{0,64},{16,80},{32,96},{48,112},{64,0},{80,16},{96,32},{112,48},{1... | collective-permute-start | bytes 6291464 | tf_op jit(solution)/shard_map/ppermute | solution.py:16
  236.8 96.9 %collective-permute-start.3 = (f32[64,8192]{1,0:T(8,128)S(1)}, f32[64,8192]{1,0:T(8,128)S(1)}, u32[]{:S(2)}, u32[]{:S(2)}) collective-permute-start(f32[64,8192]{1,0:T(8,128)S(1)} %add.50), channel_id=1, source_target_pairs={{0,128},{16,144},{32,160},{48,176},{64,192},{80,208},{96,224},{112... | collective-permute-start | bytes 6291464 | tf_op jit(solution)/shard_map/ppermute | solution.py:16
  469.5 183.4 %slice-start = ((s8[9437184]{0:T(1024)(128)(4,1)}), s8[4194304]{0:T(1024)(128)(4,1)S(1)}, s32[]{:S(2)}) async-start(s8[9437184]{0:T(1024)(128)(4,1)} %bitcast.39), calls=%async_computation | async-start | bytes 8388608
  469.5 183.4 %slice-start.1 = ((s8[9437184]{0:T(1024)(128)(4,1)}), s8[4194304]{0:T(1024)(128)(4,1)S(1)}, s32[]{:S(2)}) async-start(s8[9437184]{0:T(1024)(128)(4,1)} %bitcast.39), calls=%async_computation.1 | async-start | bytes 8388608
  475.3 33.4 %collective-permute-start.4 = (f32[64,8192]{1,0:T(8,128)S(1)}, f32[64,8192]{1,0:T(8,128)S(1)}, u32[]{:S(2)}, u32[]{:S(2)}) collective-permute-start(f32[64,8192]{1,0:T(8,128)S(1)} %fusion.20), channel_id=1, source_target_pairs={{0,16},{16,0},{32,48},{48,32},{64,80},{80,64},{96,112},{112,96},{1... | collective-permute-start | bytes 6291464 | tf_op jit(solution)/shard_map/ppermute | solution.py:16
  508.9 144.0 %slice-start.2 = ((s8[9437184]{0:T(1024)(128)(4,1)}), s8[1048576]{0:T(1024)(128)(4,1)S(1)}, s32[]{:S(2)}) async-start(s8[9437184]{0:T(1024)(128)(4,1)} %bitcast.39), calls=%async_computation.2 | async-start | bytes 2097152
  508.9 46.9 %collective-permute-start.5 = (f32[64,8192]{1,0:T(8,128)S(1)}, f32[64,8192]{1,0:T(8,128)S(1)}, u32[]{:S(2)}, u32[]{:S(2)}) collective-permute-start(f32[64,8192]{1,0:T(8,128)S(1)} %add.52), channel_id=1, source_target_pairs={{0,32},{16,48},{32,0},{48,16},{64,96},{80,112},{96,64},{112,80},{1... | collective-permute-start | bytes 6291464 | tf_op jit(solution)/shard_map/ppermute | solution.py:16
  556.0 93.0 %collective-permute-start.6 = (f32[64,8192]{1,0:T(8,128)S(1)}, f32[64,8192]{1,0:T(8,128)S(1)}, u32[]{:S(2)}, u32[]{:S(2)}) collective-permute-start(f32[64,8192]{1,0:T(8,128)S(1)} %add.53), channel_id=1, source_target_pairs={{0,64},{16,80},{32,96},{48,112},{64,0},{80,16},{96,32},{112,48},{1... | collective-permute-start | bytes 6291464 | tf_op jit(solution)/shard_map/ppermute | solution.py:16
  649.2 96.4 %collective-permute-start.7 = (f32[64,8192]{1,0:T(8,128)S(1)}, f32[64,8192]{1,0:T(8,128)S(1)}, u32[]{:S(2)}, u32[]{:S(2)}) collective-permute-start(f32[64,8192]{1,0:T(8,128)S(1)} %add.54), channel_id=1, source_target_pairs={{0,128},{16,144},{32,160},{48,176},{64,192},{80,208},{96,224},{112... | collective-permute-start | bytes 6291464 | tf_op jit(solution)/shard_map/ppermute | solution.py:16
